TPU v7x, 256 devices: a whole 4x4x8 slice. The times are simulated.
256 devices in a mesh: cols: 128 (over x, y, z), rows: 2 (over core).
Axes of the slice: x: 4, y: 4, z: 8, core: 2. Of those that a mesh axis runs over, the one named last changes fastest.
Arguments:
- activations: bfloat16 [256, 65536], P('rows', 'cols'), may hold values from 0 to 16
- weights: bfloat16 [2, 512, 40, 128, 128], P(None, 'cols', 'rows'), may hold values from -0.15625 to 0.15625
- biases: float32 [2, 65536], P(None, 'cols'), may hold values from -6 to 2
- pattern: int32 [2, 512, 40], P(None, 'cols'), may hold values from 0 to 511, as said below
- counts: int32 [2, 512], P(None, 'cols'), may hold values from 1 to 40, 10240 in all within a row
Outputs:
- result: bfloat16 [256, 65536], P('rows', 'cols')
Inputs may be any that keep to these rules, and one draw needn't show every extreme that they name: `pattern`: the 40 entries of a column block are distinct. All entries of the 4 column blocks held by one index of cols, live or not, name at most 1 different blocks among the 4 blocks held by any one index of cols, and exactly 1 for some. In each layer the counts sum to 10240.
All inputs are finite; a program needn't handle non-finite values. No bound on the sum of `counts` on one device may be relied on, other than what follows from the above.
Results may differ from a plain program's by a relative error of at most 0.0047.
Values may be sent and summed in bfloat16 or wider, within the bound.
A program may use at most 128 MiB of HBM per device.

v0:
```python
import jax
import jax.numpy as jnp
from jax import lax
from jax.sharding import PartitionSpec as P


def per_device(activations, weights, biases, pattern, counts):
    rows_here = activations.shape[0]
    owned = pattern.shape[1]
    slot_count = pattern.shape[2]
    block_size = weights.shape[-1]
    layers = weights.shape[0]
    devices = lax.axis_size("cols")
    nblocks_all = owned * devices
    current = activations
    for layer in range(layers):
        weight_all = lax.all_gather(weights[layer], "rows", axis=1, tiled=True)
        live_slots = (jnp.arange(slot_count)[None, :] < counts[layer][:, None]).astype(jnp.bfloat16)
        weight_used = weight_all * live_slots[:, :, None, None]
        layer_bias = biases[layer]
        gathered = lax.all_gather(current, "cols", axis=1, tiled=True)
        all_blocks = gathered.reshape(rows_here, nblocks_all, block_size)
        selected = jnp.take(all_blocks, pattern[layer].reshape(-1), axis=1)
        items = selected.shape[0]
        picked = selected.reshape(items, owned, slot_count, block_size)
        total = jnp.einsum(
            "sjkb,jkbc->sjc", picked, weight_used, preferred_element_type=jnp.float32
        )
        shifted = total.reshape(items, owned * block_size) + layer_bias[None, :]
        current = jnp.clip(shifted, 0.0, 32.0).astype(jnp.bfloat16)
    return current


def solution(mesh):
    return jax.shard_map(
        per_device,
        mesh=mesh,
        in_specs=(
            P("rows", "cols"),
            P(None, "cols", "rows", None, None),
            P(None, "cols"),
            P(None, "cols", None),
            P(None, "cols"),
        ),
        out_specs=P("rows", "cols"),
        check_vma=False,
    )
```

profile of v0, /device:TPU:8, one launch (start us, length us, event | category | flops | bytes accessed | tf_op | source)
XLA Modules:
  0.0 414.9 jit_solution(2486084904053249132)
XLA Ops:
  6.5 0.0 all-gather.7.cloned.1.call-start
  6.5 1.7 copy.16
  8.2 0.0 all-gather.7.cloned.1.call-update
  8.2 0.0 copy-start
  8.2 0.0 copy-start.2
  8.2 0.0 copy-start.1
  8.3 0.0 all-gather.13.cloned.1.call-start
  8.3 7.0 %fusion.10 = (bf16[1,4,20,128,128]{4,3,2,1,0:T(8,128)(2,1)}, bf16[1,4,20,128,128]{4,3,2,1,0:T(8,128)(2,1)}) fusion(bf16[2,4,20,128,128]{4,3,2,1,0:T(8,128)(2,1)} %param.8), kind=kLoop, calls=%fused_computation.28 | loop fusion | bytes 10485760 | tf_op jit(solution)/shard_map/slice | solution.py:17
  15.3 0.0 all-gather.13.cloned.1.call-update
  15.3 0.0 all-gather.9.cloned.1.call-start
  15.4 0.0 copy-done
  15.4 0.1 reshape_squeeze.6
  15.5 0.0 copy-done.2
  15.5 0.1 fusion.9
  15.6 0.0 copy-done.1
  15.6 148.4 %all-gather.7.cloned.1.call-done = bf16[128,65536]{0,1:T(8,128)(2,1)} async-done(((bf16[128,512]{0,1:T(8,128)(2,1)}), bf16[128,65536]{0,1:T(8,128)(2,1)}) %all-gather.7.cloned.1.call-update) | async-done | bytes 16777232 | tf_op jit(solution)/shard_map/all_gather | solution.py:21
  164.0 22.7 %copy.17 = bf16[128,512,128]{2,0,1:T(8,128)(2,1)} copy(bf16[128,512,128]{0,2,1:T(8,128)(2,1)} %bitcast.44) | data formatting | bytes 33554432 | tf_op jit(solution)/shard_map/reshape | solution.py:22
  186.7 13.5 %gather_fusion = bf16[160,128,128]{2,1,0:T(8,128)(2,1)} fusion(bf16[128,512,128]{2,0,1:T(8,128)(2,1)} %copy.17, s32[1024]{0:T(1024)S(1)} %pad_clamp_fusion.1), kind=kCustom, calls=%fused_computation.clone | custom fusion | bytes 10486400 | tf_op jit(solution)/shard_map/jit(_take)/gather | solution.py:23
  200.1 5.3 %broadcast_select_fusion.1 = bf16[160,128,128]{2,1,0:T(8,128)(2,1)} fusion(bf16[160,128,128]{2,1,0:T(8,128)(2,1)} %gather_fusion, pred[160]{0:T(512)(128)(4,1)S(1)} %compare_and_fusion.1), kind=kLoop, calls=%fused_computation.7 | loop fusion | flops 2621440 | bytes 10485920 | tf_op jit(solution)/shard_map/jit(_take)/select_n | solution.py:23
  205.5 0.0 all-gather.13.cloned.1.call-done
  205.5 6.1 %fusion = f32[4,128,128,1]{2,1,3,0:T(8,128)S(1)} fusion(bf16[128,4,40,128]{3,0,2,1:T(8,128)(2,1)} %bitcast.46, bf16[1,4,40,128,128]{4,3,2,1,0:T(8,128)(2,1)} %all-gather.13.cloned.1.call-done, bf16[4,40]{1,0:T(4,128)(2,1)S(1)} %fusion.9), kind=kOutput, calls=%fused_computation.3 | convolution fusion | flops 673710080 | bytes 10748224 | tf_op jit(solution)/shard_map/sjkb,jkbc->sjc/dot_general | solution.py:26
  211.6 0.8 fusion.7
  212.4 0.0 all-gather.9.cloned.1.call-update
  212.4 0.2 all-gather.11.cloned.1.call-start
  212.6 0.3 all-gather.11.cloned.1.call-update
  213.0 0.1 reshape_squeeze.7
  213.1 0.1 fusion.8
  213.2 146.7 %all-gather.9.cloned.1.call-done = bf16[128,65536]{0,1:T(8,128)(2,1)} async-done(((bf16[128,512]{0,1:T(8,128)(2,1)}), bf16[128,65536]{0,1:T(8,128)(2,1)}) %all-gather.9.cloned.1.call-update) | async-done | bytes 16777232 | tf_op jit(solution)/shard_map/all_gather | solution.py:21
  359.9 22.7 %copy.19 = bf16[128,512,128]{2,0,1:T(8,128)(2,1)} copy(bf16[128,512,128]{0,2,1:T(8,128)(2,1)} %bitcast.45) | data formatting | bytes 33554432 | tf_op jit(solution)/shard_map/reshape | solution.py:22
  382.6 13.5 %gather_fusion.1 = bf16[160,128,128]{2,1,0:T(8,128)(2,1)} fusion(bf16[128,512,128]{2,0,1:T(8,128)(2,1)} %copy.19, s32[1024]{0:T(1024)S(1)} %pad_clamp_fusion), kind=kCustom, calls=%fused_computation.1.clone | custom fusion | bytes 10486400 | tf_op jit(solution)/shard_map/jit(_take)/gather | solution.py:23
  396.0 5.3 %broadcast_select_fusion = bf16[160,128,128]{2,1,0:T(8,128)(2,1)} fusion(bf16[160,128,128]{2,1,0:T(8,128)(2,1)} %gather_fusion.1, pred[160]{0:T(512)(128)(4,1)S(1)} %compare_and_fusion), kind=kLoop, calls=%fused_computation.6 | loop fusion | flops 2621440 | bytes 10485920 | tf_op jit(solution)/shard_map/jit(_take)/select_n | solution.py:23
  401.4 0.0 all-gather.11.cloned.1.call-done
  401.4 6.1 %fusion.1 = f32[4,128,128,1]{2,1,3,0:T(8,128)S(1)} fusion(bf16[128,4,40,128]{3,0,2,1:T(8,128)(2,1)} %bitcast.47, bf16[1,4,40,128,128]{4,3,2,1,0:T(8,128)(2,1)} %all-gather.11.cloned.1.call-done, bf16[4,40]{1,0:T(4,128)(2,1)S(1)} %fusion.8), kind=kOutput, calls=%fused_computation.5 | convolution fusion | flops 673710080 | bytes 10748224 | tf_op jit(solution)/shard_map/sjkb,jkbc->sjc/dot_general | solution.py:26
  407.5 0.1 fusion.5
  407.6 0.8 copy.21
  (9 shorter events, 0.1 us)
Async XLA Ops:
  6.5 157.5 %all-gather.7.cloned.1.call-start = ((), (), s32[]{:S(2)}) async-start(), calls=%async_computation | async-start | bytes 16908288 | tf_op jit(solution)/shard_map/all_gather | solution.py:21
  8.2 7.2 %copy-start = (s32[2,4,40]{2,1,0:T(4,128)S(1)}, s32[2,4,40]{2,1,0:T(4,128)}, u32[]{:S(2)}) copy-start(s32[2,4,40]{2,1,0:T(4,128)} %param.10) | copy-start | bytes 3844
  8.2 7.3 %copy-start.2 = (s32[2,4]{1,0:T(2,128)S(1)}, s32[2,4]{1,0:T(2,128)}, u32[]{:S(2)}) copy-start(s32[2,4]{1,0:T(2,128)} %param.11) | copy-start | bytes 100
  8.2 7.4 %copy-start.1 = (f32[2,512]{1,0:T(2,128)S(1)}, f32[2,512]{1,0:T(2,128)}, u32[]{:S(2)}) copy-start(f32[2,512]{1,0:T(2,128)} %param.9) | copy-start | bytes 12292
  8.3 197.2 %all-gather.13.cloned.1.call-start = ((), (), s32[]{:S(2)}) async-start(), calls=%async_computation.3 | async-start | bytes 7864320 | tf_op jit(solution)/shard_map/all_gather | solution.py:17
  15.3 344.6 %all-gather.9.cloned.1.call-start = ((), (), s32[]{:S(2)}) async-start(), calls=%async_computation.1 | async-start | bytes 16908288 | tf_op jit(solution)/shard_map/all_gather | solution.py:21
  212.4 189.0 %all-gather.11.cloned.1.call-start = ((), (), s32[]{:S(2)}) async-start(), calls=%async_computation.2 | async-start | bytes 7864320 | tf_op jit(solution)/shard_map/all_gather | solution.py:17
Sparse Core Ops, SparseCore 0:
  11.0 152.9 all-gather.6
  165.8 17.6 all-gather.12
  212.5 147.3 all-gather.8
  361.6 17.6 all-gather.10
where the time goes:
time: 416 us; the launch traced here: 415 us
  waiting for transfers between devices  296 us (71%)
  local copies, waits for them, and re-layouts  81.9 us (20%)
  between operations  13.2 us (3%)
  matrix products  12.2 us (3%)
  other arithmetic  11.8 us (3%)
    all_gather x2, waiting for transfers between devices, per_device(): gathered = lax.all_gather(current, 'cols', axis=1, tiled=True)  295 us
    reshape x2, local copies, waits for them, and re-layouts, per_device(): all_blocks = gathered.reshape(rows_here, nblocks_all, block_size)  45.3 us
    gather x2, local copies, waits for them, and re-layouts, per_device(): selected = jnp.take(all_blocks, pattern[layer].reshape(-1), axis=1)  26.9 us
    dot_general x2, matrix products, per_device(): jnp.einsum('sjkb,jkbc->sjc', picked, weight_used, preferred_element_type=...  12.2 us
    select_n x4, other arithmetic, per_device(): selected = jnp.take(all_blocks, pattern[layer].reshape(-1), axis=1)  10.7 us
  transfers between devices with their start and end apart: 4, of which 2 were waited for; matrix products, arithmetic and copies ran while one was open for 22% of the time, Pallas kernels for 0%

commit v1 on v0

--- a/solution.py
+++ b/solution.py
@@ -1,7 +1,18 @@
+import functools
 import jax
 import jax.numpy as jnp
 from jax import lax
 from jax.sharding import PartitionSpec as P
+
+
+def _report_vector(chunk, on_dim):
+    return jnp.concatenate(
+        lax.all_to_all(jnp.stack([chunk] * lax.axis_size("cols"), axis=0), "cols", 0, 0),
+        axis=on_dim,
+    )
+
+
+supply_all_the_lanes = functools.partial(_report_vector, on_dim=1)
 
 
 def per_device(activations, weights, biases, pattern, counts):
@@ -18,7 +29,7 @@
         live_slots = (jnp.arange(slot_count)[None, :] < counts[layer][:, None]).astype(jnp.bfloat16)
         weight_used = weight_all * live_slots[:, :, None, None]
         layer_bias = biases[layer]
-        gathered = lax.all_gather(current, "cols", axis=1, tiled=True)
+        gathered = supply_all_the_lanes(current)
         all_blocks = gathered.reshape(rows_here, nblocks_all, block_size)
         selected = jnp.take(all_blocks, pattern[layer].reshape(-1), axis=1)
         items = selected.shape[0]

time: 416 us -> 888 us (2.13)
  waiting for transfers between devices: 296 us -> 719 us
  starting transfers between devices: 0.31 us -> 33.1 us
  local copies, waits for them, and re-layouts: 81.9 us -> 93.1 us
    all_to_all x0 -> x2, waiting for transfers between devices: none -> 718 us  [_report_vector(): lax.all_to_all(jnp.stack([chunk] * lax.axis_size('cols'), axis=0), 'cols'...]
    all_gather x2 -> x0, waiting for transfers between devices: 295 us -> none  [per_device(): gathered = lax.all_gather(current, 'cols', axis=1, tiled=True)]
    another operation x0 -> x4, local copies, waits for them, and re-layouts: none -> 57.6 us  [the longest x2 44.8 us: per_device(): all_blocks = gathered.reshape(rows_here, nblocks_all, block_size)]
    reshape x2, local copies, waits for them, and re-layouts: 45.3 us -> 0.27 us  [per_device(): shifted = total.reshape(items, owned * block_size) + layer_bias[None, :]]
    all_to_all x0 -> x2, starting transfers between devices: none -> 32.9 us  [_report_vector(): lax.all_to_all(jnp.stack([chunk] * lax.axis_size('cols'), axis=0), 'cols'...]
  transfers between devices with their start and end apart: 4 -> 4, of which waited for: 2 -> 2; matrix products, arithmetic and copies ran while one was open for 22% -> 10% of each run, Pallas kernels for 0% -> 0%
where the time goes in v1:
time: 888 us; the launch traced here: 882 us
  waiting for transfers between devices  719 us (81%)
  local copies, waits for them, and re-layouts  93.1 us (10%)
  starting transfers between devices  33.1 us (4%)
  between operations  13.6 us (2%)
  matrix products  12.2 us (1%)
  other arithmetic  11.6 us (1%)
    all_to_all x2, waiting for transfers between devices, _report_vector(): lax.all_to_all(jnp.stack([chunk] * lax.axis_size('cols'), axis=0), 'cols'...  718 us
    another operation x2, local copies, waits for them, and re-layouts, per_device(): all_blocks = gathered.reshape(rows_here, nblocks_all, block_size)  44.8 us
    all_to_all x2, starting transfers between devices, _report_vector(): lax.all_to_all(jnp.stack([chunk] * lax.axis_size('cols'), axis=0), 'cols'...  32.9 us
    gather x2, local copies, waits for them, and re-layouts, per_device(): selected = jnp.take(all_blocks, pattern[layer].reshape(-1), axis=1)  26.9 us
  transfers between devices with their start and end apart: 4, of which 2 were waited for; matrix products, arithmetic and copies ran while one was open for 10% of the time, Pallas kernels for 0%

profile of v1, /device:TPU:8, one launch (start us, length us, event | category | flops | bytes accessed | tf_op | source)
XLA Modules:
  0.0 882.4 jit_solution(1788812277605908067)
XLA Ops:
  6.5 1.0 copy.10
  7.6 6.4 stack.4
  14.0 15.8 %all-to-all-start = ((bf16[128,128,512]{1,2,0:T(8,128)(2,1)}), bf16[128,128,512]{1,2,0:T(8,128)(2,1)}, u32[]{:S(2)}, u32[]{:S(2)}) async-start(bf16[128,128,512]{1,2,0:T(8,128)(2,1)} %stack.4), calls=%async_computation | async-start | bytes 33554432 | tf_op jit(solution)/shard_map/all_to_all | solution.py:10
  29.8 0.0 copy-start
  29.8 0.0 copy-start.2
  29.8 0.0 copy-start.1
  29.8 0.0 all-gather.7.cloned.1.call-start
  29.9 7.0 fusion.6
  36.8 0.0 all-gather.7.cloned.1.call-update
  36.9 0.0 copy-done
  36.9 0.1 reshape_squeeze.6
  37.0 0.0 copy-done.2
  37.0 0.1 fusion.5
  37.1 0.0 copy-done.1
  37.1 356.0 %all-to-all-done = bf16[128,128,512]{1,2,0:T(8,128)(2,1)} async-done(((bf16[128,128,512]{1,2,0:T(8,128)(2,1)}), bf16[128,128,512]{1,2,0:T(8,128)(2,1)}, u32[]{:S(2)}, u32[]{:S(2)}) %all-to-all-start) | async-done | bytes 16777248 | tf_op jit(solution)/shard_map/all_to_all | solution.py:10
  393.1 22.4 %copy.11 = bf16[128,512,128]{2,0,1:T(8,128)(2,1)} copy(bf16[128,512,128]{0,2,1:T(8,128)(2,1)} %bitcast.5) | data formatting | bytes 33554432 | tf_op jit(solution)/shard_map/reshape;reshape | solution.py:33
  415.5 13.5 %gather_fusion = bf16[160,128,128]{2,1,0:T(8,128)(2,1)} fusion(bf16[128,512,128]{2,0,1:T(8,128)(2,1)} %copy.11, s32[1024]{0:T(1024)S(1)} %pad_clamp_fusion.1), kind=kCustom, calls=%fused_computation.clone | custom fusion | bytes 10486400 | tf_op jit(solution)/shard_map/jit(_take)/gather | solution.py:34
  429.0 5.3 broadcast_select_fusion.1
  434.3 0.0 all-gather.7.cloned.1.call-done
  434.3 6.1 fusion
  440.4 0.1 copy.13
  440.6 0.1 copy.14
  440.7 6.4 stack.5
  447.1 17.1 %all-to-all-start.1 = ((bf16[128,128,512]{1,2,0:T(8,128)(2,1)}), bf16[128,128,512]{1,2,0:T(8,128)(2,1)}, u32[]{:S(2)}, u32[]{:S(2)}) async-start(bf16[128,128,512]{1,2,0:T(8,128)(2,1)} %stack.5), calls=%async_computation.1 | async-start | bytes 33554432 | tf_op jit(solution)/shard_map/all_to_all | solution.py:10
  464.2 0.2 all-gather.5.cloned.1.call-start
  464.4 0.5 all-gather.5.cloned.1.call-update
  464.9 0.1 reshape_squeeze.7
  465.0 0.1 fusion.4
  465.1 362.3 %all-to-all-done.1 = bf16[128,128,512]{1,2,0:T(8,128)(2,1)} async-done(((bf16[128,128,512]{1,2,0:T(8,128)(2,1)}), bf16[128,128,512]{1,2,0:T(8,128)(2,1)}, u32[]{:S(2)}, u32[]{:S(2)}) %all-to-all-start.1) | async-done | bytes 16777248 | tf_op jit(solution)/shard_map/all_to_all | solution.py:10
  827.4 22.4 %copy.15 = bf16[128,512,128]{2,0,1:T(8,128)(2,1)} copy(bf16[128,512,128]{0,2,1:T(8,128)(2,1)} %bitcast.14) | data formatting | bytes 33554432 | tf_op jit(solution)/shard_map/reshape;reshape | solution.py:33
  849.8 13.5 %gather_fusion.1 = bf16[160,128,128]{2,1,0:T(8,128)(2,1)} fusion(bf16[128,512,128]{2,0,1:T(8,128)(2,1)} %copy.15, s32[1024]{0:T(1024)S(1)} %pad_clamp_fusion), kind=kCustom, calls=%fused_computation.1.clone | custom fusion | bytes 10486400 | tf_op jit(solution)/shard_map/jit(_take)/gather | solution.py:34
  863.3 5.3 broadcast_select_fusion
  868.6 0.0 all-gather.5.cloned.1.call-done
  868.6 6.1 fusion.1
  874.7 0.1 copy.17
  874.9 0.7 clamp_convert_fusion
  (10 shorter events, 0.1 us)
Async XLA Ops:
  14.0 379.1 %all-to-all-start = ((bf16[128,128,512]{1,2,0:T(8,128)(2,1)}), bf16[128,128,512]{1,2,0:T(8,128)(2,1)}, u32[]{:S(2)}, u32[]{:S(2)}) async-start(bf16[128,128,512]{1,2,0:T(8,128)(2,1)} %stack.4), calls=%async_computation | async-start | bytes 33554432 | tf_op jit(solution)/shard_map/all_to_all | solution.py:10
  29.8 7.1 copy-start
  29.8 7.2 copy-start.2
  29.8 7.3 copy-start.1
  29.8 404.5 %all-gather.7.cloned.1.call-start = ((), (), s32[]{:S(2)}) async-start(), calls=%async_computation.3 | async-start | bytes 7864320 | tf_op jit(solution)/shard_map/all_gather | solution.py:28
  447.1 380.3 %all-to-all-start.1 = ((bf16[128,128,512]{1,2,0:T(8,128)(2,1)}), bf16[128,128,512]{1,2,0:T(8,128)(2,1)}, u32[]{:S(2)}, u32[]{:S(2)}) async-start(bf16[128,128,512]{1,2,0:T(8,128)(2,1)} %stack.5), calls=%async_computation.1 | async-start | bytes 33554432 | tf_op jit(solution)/shard_map/all_to_all | solution.py:10
  464.2 404.5 %all-gather.5.cloned.1.call-start = ((), (), s32[]{:S(2)}) async-start(), calls=%async_computation.2 | async-start | bytes 7864320 | tf_op jit(solution)/shard_map/all_gather | solution.py:28
Sparse Core Ops, SparseCore 0:
  37.0 21.8 all-gather.6
  466.8 21.8 all-gather.4
